TPU v7x, 512 devices: a whole 4x8x8 slice. The times are simulated.
512 devices in a mesh: fsdp: 64 (over y, x, core), cent: 8 (over z).
Axes of the slice: x: 4, y: 8, z: 8, core: 2. Of those that a mesh axis runs over, the one named last changes fastest.
Arguments:
- attention: bfloat16 [8192, 4096], P('fsdp', 'cent'), may hold values from -6 to 6
- w_out: bfloat16 [4096, 4096], P('cent', 'fsdp'), may hold values from -0.09375 to 0.09375
- hidden: bfloat16 [8192, 4096], P(('fsdp', 'cent')), may hold values from -6 to 6
- norm_gain: bfloat16 [4096], replicated, may hold values from 0.099609375 to 1.8984375
- centroids: bfloat16 [512, 4096], P('cent'), may hold values from -3 to 3
- token_codes: int32 [8192], P(('fsdp', 'cent')), may hold values from 0 to 63, as said below
- tile_lists: int32 [64, 8], P('fsdp'), may hold values from 0 to 63, as said below
Outputs:
- centroid_sums: float32 [512, 4096], P('cent', 'fsdp')
- residual_gram: float32 [4096, 4096], P('fsdp', 'cent')
Inputs may be any that keep to these rules, and one draw needn't show every extreme that they name: `token_codes`: token t belongs to block t // 128; its code k names centroid k % 8 of the tile at slot k // 8 of that block's list; every slot of a block's list is used. `tile_lists`: each row holds 8 distinct tile ids in ascending order; tile j holds centroids j * 8 to j * 8 + 7, and centroid g belongs to owner shard g // 64; in every row at most 2 listed tiles share an owner, and exactly 2 do for some owner.
All inputs are finite; a program needn't handle non-finite values.
Results may differ from a plain program's by a relative error of at most 0.0085.
Values may be sent and summed in bfloat16 or wider, within the bound.
A program may use at most 64 MiB of HBM per device.

v0:
```python
import jax
import jax.numpy as jnp
from jax import lax
from jax.sharding import PartitionSpec as P

TILE = 8
LT = 8


def shards(attention, w_out, hidden, norm_gain, centroids, token_codes, tile_lists):
    tok_dev = hidden.shape[0]
    feat_dim = hidden.shape[1]
    n_fsdp = lax.axis_size("fsdp")
    n_cent = lax.axis_size("cent")
    cap_slots = max(2, 2 * LT // n_cent)
    partial_out = jnp.dot(
        attention,
        lax.all_gather(w_out, "fsdp", axis=1, tiled=True),
        preferred_element_type=jnp.float32,
    )
    head_sum = lax.psum_scatter(
        partial_out.astype(jnp.bfloat16), "cent", scatter_dimension=0, tiled=True
    ).astype(jnp.float32)
    mixed_rows = hidden.astype(jnp.float32) + head_sum
    normed = (
        mixed_rows
        * lax.rsqrt(jnp.mean(mixed_rows * mixed_rows, axis=1, keepdims=True) + 1e-05)
        * norm_gain.astype(jnp.float32)
    )
    cent_dev = centroids.shape[0]
    own_tiles = cent_dev // TILE
    owner_idx = lax.axis_index("cent")
    listed = tile_lists[0]
    local_tile = listed - owner_idx * own_tiles
    owned_here = (local_tile >= 0) & (local_tile < own_tiles)
    safe_tile = jnp.clip(local_tile, 0, own_tiles - 1)
    tiles_here = centroids.reshape(own_tiles, TILE, feat_dim)
    slot_of = token_codes // TILE
    offset = token_codes % TILE
    rank_mine = jnp.cumsum(owned_here.astype(jnp.int32)) - 1
    chosen = owned_here[None, :] & (
        rank_mine[None, :] == jnp.arange(cap_slots, dtype=jnp.int32)[:, None]
    )
    send_tile = jnp.sum(jnp.where(chosen, safe_tile[None, :], 0), axis=1)
    filled = jnp.any(chosen, axis=1)
    outgoing = jnp.where(
        filled[:, None, None],
        jnp.take(tiles_here, send_tile, axis=0),
        jnp.zeros((cap_slots, TILE, feat_dim), jnp.bfloat16),
    )
    arrived = lax.all_gather(outgoing, "cent", axis=0, tiled=True)
    owner_of = listed // own_tiles
    list_pos = jnp.arange(LT, dtype=jnp.int32)
    earlier = (owner_of[None, :] == owner_of[:, None]) & (list_pos[None, :] < list_pos[:, None])
    rank_all = jnp.sum(earlier.astype(jnp.int32), axis=1)
    where_tile = owner_of * cap_slots + rank_all
    tile_rows = arrived.reshape(-1, feat_dim)
    centers = jnp.take(tile_rows, where_tile[slot_of] * TILE + offset, axis=0)
    residual = (normed - centers.astype(jnp.float32)).astype(jnp.bfloat16)
    onehot = (token_codes[None, :] == jnp.arange(LT * TILE, dtype=jnp.int32)[:, None]).astype(
        jnp.bfloat16
    )
    slot_part = jnp.dot(onehot, residual, preferred_element_type=jnp.float32)
    slot_sum = lax.psum(slot_part.astype(jnp.bfloat16), "cent").astype(jnp.float32)
    target = (local_tile[:, None] * TILE + jnp.arange(TILE, dtype=jnp.int32)[None, :]).reshape(-1)
    valid_rows = jnp.repeat(owned_here, TILE)
    placer = (
        (jnp.arange(cent_dev, dtype=jnp.int32)[:, None] == target[None, :]) & valid_rows[None, :]
    ).astype(jnp.float32)
    dense_part = jnp.dot(
        placer, slot_sum, precision=lax.Precision.HIGHEST, preferred_element_type=jnp.float32
    )
    centroid_sums = lax.psum_scatter(dense_part, "fsdp", scatter_dimension=1, tiled=True)
    rows_dev = feat_dim // n_fsdp
    row_start = lax.axis_index("fsdp") * rows_dev
    shard_rows = lax.all_gather(residual, "fsdp", axis=0, tiled=True)
    left_cols = lax.dynamic_slice_in_dim(shard_rows, row_start, rows_dev, 1)
    gram_part = lax.dot_general(
        left_cols, shard_rows, (((0,), (0,)), ((), ())), preferred_element_type=jnp.float32
    )
    gram_sum = lax.psum_scatter(gram_part, "cent", scatter_dimension=1, tiled=True)
    tokens_all = tok_dev * n_fsdp * n_cent
    return (centroid_sums, gram_sum / tokens_all)


def solution(mesh):
    in_specs = (
        P("fsdp", "cent"),
        P("cent", "fsdp"),
        P(("fsdp", "cent"), None),
        P(),
        P("cent", None),
        P(("fsdp", "cent")),
        P("fsdp", None),
    )
    out_specs = (P("cent", "fsdp"), P("fsdp", "cent"))
    return jax.shard_map(shards, mesh=mesh, in_specs=in_specs, out_specs=out_specs, check_vma=False)
```

profile of v0, /device:TPU:2, one launch (start us, length us, event | category | flops | bytes accessed | tf_op | source)
XLA Modules:
  0.0 561.0 jit_solution(6380447563696765636)
XLA Ops:
  7.3 0.7 all-gather.4.cloned.1.call-update
  8.0 0.7 convert_bitcast_fusion
  8.7 0.2 reduce-window.8
  8.9 0.7 fusion.11
  9.5 0.1 select_reduce_fusion
  9.7 0.6 gather_fusion.1
  10.2 0.1 fusion.8
  10.4 0.7 select_select_fusion
  11.2 88.0 %all-gather.4.cloned.1.call-done = bf16[512,4096]{0,1:T(8,128)(2,1)} async-done(((bf16[512,64]{0,1:T(8,128)(2,1)}), bf16[512,4096]{0,1:T(8,128)(2,1)}) %all-gather.4.cloned.1.call-update) | async-done | bytes 4194320 | tf_op jit(solution)/shard_map/all_gather | solution.py:18
  99.2 4.8 convolution_convert_fusion
  104.0 0.0 all-reduce.2.cloned.1.call-start
  104.1 0.2 convert_reduce_fusion
  104.3 0.7 gather_fusion
  105.0 37.3 %all-gather.6.cloned.1.call-done = bf16[16,8,4096]{2,1,0:T(8,128)(2,1)} async-done(((bf16[2,8,4096]{2,1,0:T(8,128)(2,1)}), bf16[16,8,4096]{2,1,0:T(8,128)(2,1)}) %all-gather.6.cloned.1.call-update) | async-done | bytes 1048592 | tf_op jit(solution)/shard_map/all_gather | solution.py:51
  142.4 2.1 gather_fusion.2
  144.5 41.3 %reduce-scatter.6.cloned.1.call-done = bf16[16,4096]{1,0:T(8,128)(2,1)} async-done(((bf16[128,4096]{1,0:T(8,128)(2,1)}), bf16[16,4096]{1,0:T(8,128)(2,1)}) %reduce-scatter.6.cloned.1.call-update) | async-done | bytes 131088 | tf_op jit(solution)/shard_map/reduce_scatter | solution.py:21
  185.8 1.1 multiply_reduce_fusion
  186.9 1.0 subtract_convert_fusion
  187.9 1.1 convolution_convert_fusion.1
  189.1 0.5 all-gather.8.cloned.1.call-update
  189.7 0.1 iota_add_fusion
  189.8 0.1 add.94
  189.9 0.1 broadcast_in_dim.69
  190.0 0.1 and.75
  190.1 77.2 %all-reduce.2.cloned.1.call-done = bf16[64,4096]{1,0:T(8,128)(2,1)} async-done(((bf16[64,4096]{1,0:T(8,128)(2,1)}), bf16[64,4096]{1,0:T(8,128)(2,1)}) %all-reduce.2.cloned.1.call-update) | async-done | bytes 524304 | tf_op jit(solution)/shard_map/psum | solution.py:64
  267.3 2.9 convolution_bitcast_fusion
  270.3 85.8 %all-gather.8.cloned.1.call-done = bf16[1024,4096]{1,0:T(8,128)(2,1)} async-done(((bf16[16,4096]{1,0:T(8,128)(2,1)}), bf16[1024,4096]{1,0:T(8,128)(2,1)}) %all-gather.8.cloned.1.call-update) | async-done | bytes 8388624 | tf_op jit(solution)/shard_map/all_gather | solution.py:76
  356.1 6.1 %fusion = f32[64,4096]{1,0:T(8,128)} fusion(bf16[1024,4096]{1,0:T(8,128)(2,1)} %all-gather.8.cloned.1.call-done, s32[]{:T(128)S(6)} %select_n.78), kind=kOutput, calls=%fused_computation.6 | convolution fusion | flops 536870912 | bytes 9699332 | tf_op jit(solution)/shard_map/dot_general | solution.py:78
  362.3 145.4 %reduce-scatter.10.cloned.1.call-done = f32[64,64]{1,0:T(8,128)} async-done(((f32[4096,64]{1,0:T(8,128)}), f32[64,64]{1,0:T(8,128)}) %reduce-scatter.10.cloned.1.call-update) | async-done | bytes 16400
  507.7 1.5 copy.10
  509.1 43.5 %reduce-scatter.8.cloned.1.call-done = f32[64,512]{1,0:T(8,128)} async-done(((f32[64,4096]{1,0:T(8,128)}), f32[64,512]{1,0:T(8,128)}) %reduce-scatter.8.cloned.1.call-update) | async-done | bytes 131088 | tf_op jit(solution)/shard_map/reduce_scatter | solution.py:81
  552.6 1.6 broadcast_multiply_fusion
  (36 shorter events, 0.5 us)
Async XLA Ops:
  7.2 2.5 copy-start
  7.2 96.9 %copy-start.4 = (s32[1,8]{1,0:T(1,128)S(1)}, s32[1,8]{1,0:T(1,128)}, u32[]{:S(2)}) copy-start(s32[1,8]{1,0:T(1,128)} %param.13) | copy-start | bytes 100
  7.2 96.9 %copy-start.3 = (bf16[4096]{0:T(1024)(128)(2,1)S(1)}, bf16[4096]{0:T(1024)(128)(2,1)}, u32[]{:S(2)}) copy-start(bf16[4096]{0:T(1024)(128)(2,1)} %param.10) | copy-start | bytes 24580
  7.2 96.9 %copy-start.5 = (s32[16]{0:T(128)S(1)}, s32[16]{0:T(128)}, u32[]{:S(2)}) copy-start(s32[16]{0:T(128)} %param.12) | copy-start | bytes 196
  7.2 92.0 %all-gather.4.cloned.1.call-start = ((), (), s32[]{:S(2)}) async-start(), calls=%async_computation.3 | async-start | bytes 4259840 | tf_op jit(solution)/shard_map/all_gather | solution.py:18
  7.9 134.4 %all-gather.6.cloned.1.call-start = ((), (), s32[]{:S(2)}) async-start(), calls=%async_computation.5 | async-start | bytes 1179648 | tf_op jit(solution)/shard_map/all_gather | solution.py:51
  11.1 174.7 %copy-start.2 = (bf16[16,4096]{1,0:T(8,128)(2,1)S(1)}, bf16[16,4096]{1,0:T(8,128)(2,1)}, u32[]{:S(2)}) copy-start(bf16[16,4096]{1,0:T(8,128)(2,1)} %param.9) | copy-start | bytes 393220
  11.1 174.7 %reduce-scatter.6.cloned.1.call-start = ((), (), s32[]{:S(2)}) async-start(), calls=%async_computation.4 | async-start | bytes 1179648 | tf_op jit(solution)/shard_map/reduce_scatter | solution.py:21
  104.0 163.3 %all-reduce.2.cloned.1.call-start = ((), (), s32[]{:S(2)}) async-start(), calls=%async_computation.6 | async-start | bytes 1048576 | tf_op jit(solution)/shard_map/psum | solution.py:64
  187.9 1.2 copy-start.1
  189.1 167.0 %all-gather.8.cloned.1.call-start = ((), (), s32[]{:S(2)}) async-start(), calls=%async_computation.7 | async-start | bytes 8519680 | tf_op jit(solution)/shard_map/all_gather | solution.py:76
  189.7 318.0 %reduce-scatter.10.cloned.1.call-start = ((), (), s32[]{:S(2)}) async-start(), calls=%async_computation.9 | async-start | bytes 2129920
  270.2 282.3 %reduce-scatter.8.cloned.1.call-start = ((), (), s32[]{:S(2)}) async-start(), calls=%async_computation.8 | async-start | bytes 1179648 | tf_op jit(solution)/shard_map/reduce_scatter | solution.py:81
Sparse Core Ops, SparseCore 0:
  11.4 87.8 all-gather.3
  101.9 40.4 all-gather.5
  145.2 40.5 reduce-scatter.5
  189.2 78.0 all-reduce.1
  271.1 84.9 all-gather.7
  360.6 147.0 reduce-scatter.9
  510.5 42.0 reduce-scatter.7
where the time goes:
time: 561 us
  waiting for transfers between devices  520 us (93%)
  matrix products  15 us (3%)
  between operations  14.3 us (3%)
  other arithmetic  6.51 us (1%)
    unnamed x8, waiting for transfers between devices  147 us
    all_gather x1, waiting for transfers between devices, shards(): lax.all_gather(w_out, 'fsdp', axis=1, tiled=True)  88 us
    all_gather x1, waiting for transfers between devices, shards(): shard_rows = lax.all_gather(residual, 'fsdp', axis=0, tiled=True)  85.8 us
    psum x1, waiting for transfers between devices, shards(): lax.psum(slot_part.astype(jnp.bfloat16), 'cent').astype(jnp.float32)  77.2 us
    reduce_scatter x1, waiting for transfers between devices, shards(): lax.psum_scatter(gram_part, 'cent', scatter_dimension=1, tiled=True)  43.5 us
    reduce_scatter x1, waiting for transfers between devices, shards(): lax.psum_scatter(partial_out.astype(jnp.bfloat16), 'cent', scatter_dimens...  41.3 us
    all_gather x1, waiting for transfers between devices, shards(): arrived = lax.all_gather(outgoing, 'cent', axis=0, tiled=True)  37.3 us
  transfers between devices with their start and end apart: 7, of which 7 were waited for; matrix products, arithmetic and copies ran while one was open for 4% of the time, Pallas kernels for 0%

commit v1 on v0

--- a/solution.py
+++ b/solution.py
@@ -5,6 +5,22 @@
 
 TILE = 8
 LT = 8
+
+
+def collect(x, axis, dim):
+    ways, here, step = (lax.axis_size(axis), lax.axis_index(axis), x.shape[dim])
+    dims = [n * ways if d == dim else n for d, n in enumerate(x.shape)]
+    full = lax.dynamic_update_slice_in_dim(jnp.zeros(dims, x.dtype), x, here * step, axis=dim)
+    going_up = going_down = x
+    for far in range(1, ways // 2 + 1):
+        going_up = lax.ppermute(going_up, axis, [(d, (d + 1) % ways) for d in range(ways)])
+        full = lax.dynamic_update_slice_in_dim(full, going_up, (here - far) % ways * step, axis=dim)
+        if 2 * far < ways:
+            going_down = lax.ppermute(going_down, axis, [(d, (d - 1) % ways) for d in range(ways)])
+            full = lax.dynamic_update_slice_in_dim(
+                full, going_down, (here + far) % ways * step, axis=dim
+            )
+    return full
 
 
 def shards(attention, w_out, hidden, norm_gain, centroids, token_codes, tile_lists):
@@ -48,7 +64,7 @@
         jnp.take(tiles_here, send_tile, axis=0),
         jnp.zeros((cap_slots, TILE, feat_dim), jnp.bfloat16),
     )
-    arrived = lax.all_gather(outgoing, "cent", axis=0, tiled=True)
+    arrived = collect(outgoing, "cent", 0)
     owner_of = listed // own_tiles
     list_pos = jnp.arange(LT, dtype=jnp.int32)
     earlier = (owner_of[None, :] == owner_of[:, None]) & (list_pos[None, :] < list_pos[:, None])

time: 561 us -> 521 us (0.929)
  waiting for transfers between devices: 520 us -> 448 us
  starting transfers between devices: 0.28 us -> 30.8 us
    all_gather x1 -> x0, waiting for transfers between devices: 37.3 us -> none  [shards(): arrived = lax.all_gather(outgoing, 'cent', axis=0, tiled=True)]
    all_gather x1, waiting for transfers between devices: 88 us -> 56.9 us  [shards(): lax.all_gather(w_out, 'fsdp', axis=1, tiled=True)]
    ppermute x0 -> x7, starting transfers between devices: none -> 30.5 us  [the longest x3 18.9 us: collect(): lax.ppermute(going_down, axis, [(d, (d - 1) % ways) for d in range(ways)])]
    reduce_scatter x1, waiting for transfers between devices: 41.3 us -> 30.7 us  [shards(): lax.psum_scatter(partial_out.astype(jnp.bfloat16), 'cent', scatter_dimens...]
    ppermute x0 -> x7, waiting for transfers between devices: none -> 7.04 us  [the longest x4 7.03 us: collect(): lax.ppermute(going_up, axis, [(d, (d + 1) % ways) for d in range(ways)])]
    unnamed x8 -> x7, waiting for transfers between devices: 147 us -> 147 us
  transfers between devices with their start and end apart: 7 -> 13, of which waited for: 7 -> 8; matrix products, arithmetic and copies ran while one was open for 4% -> 4% of each run, Pallas kernels for 0% -> 0%
where the time goes in v1:
time: 521 us; the launch traced here: 520 us
  waiting for transfers between devices  448 us (86%)
  starting transfers between devices  30.8 us (6%)
  matrix products  14.9 us (3%)
  between operations  14.5 us (3%)
  other arithmetic  8.54 us (2%)
    unnamed x7, waiting for transfers between devices  147 us
    all_gather x1, waiting for transfers between devices, shards(): shard_rows = lax.all_gather(residual, 'fsdp', axis=0, tiled=True)  85.8 us
    psum x1, waiting for transfers between devices, shards(): lax.psum(slot_part.astype(jnp.bfloat16), 'cent').astype(jnp.float32)  77.2 us
    all_gather x1, waiting for transfers between devices, shards(): lax.all_gather(w_out, 'fsdp', axis=1, tiled=True)  56.9 us
    reduce_scatter x1, waiting for transfers between devices, shards(): lax.psum_scatter(gram_part, 'cent', scatter_dimension=1, tiled=True)  43.4 us
    reduce_scatter x1, waiting for transfers between devices, shards(): lax.psum_scatter(partial_out.astype(jnp.bfloat16), 'cent', scatter_dimens...  30.7 us
    ppermute x3, starting transfers between devices, collect(): lax.ppermute(going_down, axis, [(d, (d - 1) % ways) for d in range(ways)])  18.9 us
    ppermute x4, starting transfers between devices, collect(): lax.ppermute(going_up, axis, [(d, (d + 1) % ways) for d in range(ways)])  11.7 us
  transfers between devices with their start and end apart: 13, of which 8 were waited for; matrix products, arithmetic and copies ran while one was open for 4% of the time, Pallas kernels for 0%

profile of v1, /device:TPU:2, one launch (start us, length us, event | category | flops | bytes accessed | tf_op | source)
XLA Modules:
  0.0 520.2 jit_solution(4463569754238815156)
XLA Ops:
  7.2 0.7 all-gather.3.cloned.1.call-update
  8.0 0.7 convert_bitcast_fusion
  8.8 0.7 fusion.12
  10.5 4.3 collective-permute-start
  14.8 8.6 %collective-permute-start.1 = (bf16[2,8,4096]{2,1,0:T(8,128)(2,1)S(1)}, bf16[2,8,4096]{2,1,0:T(8,128)(2,1)S(1)}, u32[]{:S(2)}, u32[]{:S(2)}) collective-permute-start(bf16[2,8,4096]{2,1,0:T(8,128)(2,1)S(1)} %get-tuple-element.5), channel_id=1, source_target_pairs={{0,7},{1,0},{2,1},{3,2},{4,3},{5,4},{6,5},{7,6},{8,15},{9,8},{10,9... | collective-permute-start | bytes 393224 | tf_op jit(solution)/shard_map/ppermute | solution.py:19
  23.4 0.7 compare_select_fusion.3
  24.1 0.7 fusion.13
  24.9 0.7 gather_fusion
  25.6 0.7 compare_and_fusion.3
  26.4 0.7 convert_element_type.35
  27.1 1.9 collective-permute-start.2
  29.1 5.1 collective-permute-start.3
  34.3 0.9 collective-permute-done.2
  35.2 1.9 collective-permute-start.4
  37.1 5.1 collective-permute-start.5
  42.3 56.9 %all-gather.3.cloned.1.call-done = bf16[512,4096]{0,1:T(8,128)(2,1)} async-done(((bf16[512,64]{0,1:T(8,128)(2,1)}), bf16[512,4096]{0,1:T(8,128)(2,1)}) %all-gather.3.cloned.1.call-update) | async-done | bytes 4194320 | tf_op jit(solution)/shard_map/all_gather | solution.py:34
  99.2 4.7 convolution_convert_fusion
  104.0 3.6 collective-permute-start.6
  107.7 6.1 %collective-permute-done.6 = bf16[2,8,4096]{2,1,0:T(8,128)(2,1)S(1)} collective-permute-done((bf16[2,8,4096]{2,1,0:T(8,128)(2,1)S(1)}, bf16[2,8,4096]{2,1,0:T(8,128)(2,1)S(1)}, u32[]{:S(2)}, u32[]{:S(2)}) %collective-permute-start.6) | collective-permute-done | bytes 131104 | tf_op jit(solution)/shard_map/ppermute | solution.py:16
  113.8 0.6 gather_fusion.2
  114.4 30.7 %reduce-scatter.6.cloned.1.call-done = bf16[16,4096]{1,0:T(8,128)(2,1)} async-done(((bf16[128,4096]{1,0:T(8,128)(2,1)}), bf16[16,4096]{1,0:T(8,128)(2,1)}) %reduce-scatter.6.cloned.1.call-update) | async-done | bytes 131088 | tf_op jit(solution)/shard_map/reduce_scatter | solution.py:37
  145.1 1.1 multiply_reduce_fusion
  146.2 1.0 subtract_convert_fusion
  147.2 1.1 convolution_convert_fusion.1
  149.3 77.2 %all-reduce.2.cloned.1.call-done = bf16[64,4096]{1,0:T(8,128)(2,1)} async-done(((bf16[64,4096]{1,0:T(8,128)(2,1)}), bf16[64,4096]{1,0:T(8,128)(2,1)}) %all-reduce.2.cloned.1.call-update) | async-done | bytes 524304 | tf_op jit(solution)/shard_map/psum | solution.py:80
  226.6 2.9 convolution_bitcast_fusion
  229.6 85.8 %all-gather.5.cloned.1.call-done = bf16[1024,4096]{1,0:T(8,128)(2,1)} async-done(((bf16[16,4096]{1,0:T(8,128)(2,1)}), bf16[1024,4096]{1,0:T(8,128)(2,1)}) %all-gather.5.cloned.1.call-update) | async-done | bytes 8388624 | tf_op jit(solution)/shard_map/all_gather | solution.py:92
  315.4 6.2 %fusion = f32[64,4096]{1,0:T(8,128)} fusion(bf16[1024,4096]{1,0:T(8,128)(2,1)} %all-gather.5.cloned.1.call-done, s32[]{:T(128)S(6)} %select_n.147), kind=kOutput, calls=%fused_computation.6 | convolution fusion | flops 536870912 | bytes 9699332 | tf_op jit(solution)/shard_map/dot_general | solution.py:94
  321.6 145.4 %reduce-scatter.10.cloned.1.call-done = f32[64,64]{1,0:T(8,128)} async-done(((f32[4096,64]{1,0:T(8,128)}), f32[64,64]{1,0:T(8,128)}) %reduce-scatter.10.cloned.1.call-update) | async-done | bytes 16400
  466.9 1.5 copy.10
  468.4 43.4 %reduce-scatter.8.cloned.1.call-done = f32[64,512]{1,0:T(8,128)} async-done(((f32[64,4096]{1,0:T(8,128)}), f32[64,512]{1,0:T(8,128)}) %reduce-scatter.8.cloned.1.call-update) | async-done | bytes 131088 | tf_op jit(solution)/shard_map/reduce_scatter | solution.py:97
  511.7 1.6 broadcast_multiply_fusion
  (53 shorter events, 2.7 us)
Async XLA Ops:
  7.2 2.5 copy-start
  7.2 92.0 %all-gather.3.cloned.1.call-start = ((), (), s32[]{:S(2)}) async-start(), calls=%async_computation.3 | async-start | bytes 4259840 | tf_op jit(solution)/shard_map/all_gather | solution.py:34
  7.9 137.2 %reduce-scatter.6.cloned.1.call-start = ((), (), s32[]{:S(2)}) async-start(), calls=%async_computation.4 | async-start | bytes 1179648 | tf_op jit(solution)/shard_map/reduce_scatter | solution.py:37
  10.5 16.6 %collective-permute-start = (bf16[2,8,4096]{2,1,0:T(8,128)(2,1)S(1)}, bf16[2,8,4096]{2,1,0:T(8,128)(2,1)S(1)}, u32[]{:S(2)}, u32[]{:S(2)}) collective-permute-start(bf16[2,8,4096]{2,1,0:T(8,128)(2,1)S(1)} %get-tuple-element.5), channel_id=1, source_target_pairs={{0,1},{1,2},{2,3},{3,4},{4,5},{5,6},{6,7},{7,0},{8,9},{9,10},{10,1... | collective-permute-start | bytes 393224 | tf_op jit(solution)/shard_map/ppermute | solution.py:16
  14.8 14.2 %collective-permute-start.1 = (bf16[2,8,4096]{2,1,0:T(8,128)(2,1)S(1)}, bf16[2,8,4096]{2,1,0:T(8,128)(2,1)S(1)}, u32[]{:S(2)}, u32[]{:S(2)}) collective-permute-start(bf16[2,8,4096]{2,1,0:T(8,128)(2,1)S(1)} %get-tuple-element.5), channel_id=1, source_target_pairs={{0,7},{1,0},{2,1},{3,2},{4,3},{5,4},{6,5},{7,6},{8,15},{9,8},{10,9... | collective-permute-start | bytes 393224 | tf_op jit(solution)/shard_map/ppermute | solution.py:19
  27.1 8.1 %collective-permute-start.2 = (bf16[2,8,4096]{2,1,0:T(8,128)(2,1)S(1)}, bf16[2,8,4096]{2,1,0:T(8,128)(2,1)S(1)}, u32[]{:S(2)}, u32[]{:S(2)}) collective-permute-start(bf16[2,8,4096]{2,1,0:T(8,128)(2,1)S(1)} %collective-permute-done), channel_id=1, source_target_pairs={{0,1},{1,2},{2,3},{3,4},{4,5},{5,6},{6,7},{7,0},{8,9},{9,10},{10,1... | collective-permute-start | bytes 393224 | tf_op jit(solution)/shard_map/ppermute | solution.py:16
  29.1 8.1 %collective-permute-start.3 = (bf16[2,8,4096]{2,1,0:T(8,128)(2,1)S(1)}, bf16[2,8,4096]{2,1,0:T(8,128)(2,1)S(1)}, u32[]{:S(2)}, u32[]{:S(2)}) collective-permute-start(bf16[2,8,4096]{2,1,0:T(8,128)(2,1)S(1)} %collective-permute-done.1), channel_id=1, source_target_pairs={{0,7},{1,0},{2,1},{3,2},{4,3},{5,4},{6,5},{7,6},{8,15},{9,8},{10,9... | collective-permute-start | bytes 393224 | tf_op jit(solution)/shard_map/ppermute | solution.py:19
  34.2 110.9 %copy-start.2 = (bf16[16,4096]{1,0:T(8,128)(2,1)S(1)}, bf16[16,4096]{1,0:T(8,128)(2,1)}, u32[]{:S(2)}) copy-start(bf16[16,4096]{1,0:T(8,128)(2,1)} %param.9) | copy-start | bytes 393220
  34.3 113.0 %copy-start.4 = (s32[16]{0:T(128)S(1)}, s32[16]{0:T(128)}, u32[]{:S(2)}) copy-start(s32[16]{0:T(128)} %param.12) | copy-start | bytes 196
  34.3 114.9 %copy-start.3 = (s32[1,8]{1,0:T(1,128)S(1)}, s32[1,8]{1,0:T(1,128)}, u32[]{:S(2)}) copy-start(s32[1,8]{1,0:T(1,128)} %param.13) | copy-start | bytes 100
  35.2 68.8 %collective-permute-start.4 = (bf16[2,8,4096]{2,1,0:T(8,128)(2,1)S(1)}, bf16[2,8,4096]{2,1,0:T(8,128)(2,1)S(1)}, u32[]{:S(2)}, u32[]{:S(2)}) collective-permute-start(bf16[2,8,4096]{2,1,0:T(8,128)(2,1)S(1)} %collective-permute-done.2), channel_id=1, source_target_pairs={{0,1},{1,2},{2,3},{3,4},{4,5},{5,6},{6,7},{7,0},{8,9},{9,10},{10,1... | collective-permute-start | bytes 393224 | tf_op jit(solution)/shard_map/ppermute | solution.py:16
  37.1 70.5 %collective-permute-start.5 = (bf16[2,8,4096]{2,1,0:T(8,128)(2,1)S(1)}, bf16[2,8,4096]{2,1,0:T(8,128)(2,1)S(1)}, u32[]{:S(2)}, u32[]{:S(2)}) collective-permute-start(bf16[2,8,4096]{2,1,0:T(8,128)(2,1)S(1)} %collective-permute-done.3), channel_id=1, source_target_pairs={{0,7},{1,0},{2,1},{3,2},{4,3},{5,4},{6,5},{7,6},{8,15},{9,8},{10,9... | collective-permute-start | bytes 393224 | tf_op jit(solution)/shard_map/ppermute | solution.py:19
  103.9 122.7 %all-reduce.2.cloned.1.call-start = ((), (), s32[]{:S(2)}) async-start(), calls=%async_computation.5 | async-start | bytes 1048576 | tf_op jit(solution)/shard_map/psum | solution.py:80
  104.0 9.8 %collective-permute-start.6 = (bf16[2,8,4096]{2,1,0:T(8,128)(2,1)S(1)}, bf16[2,8,4096]{2,1,0:T(8,128)(2,1)S(1)}, u32[]{:S(2)}, u32[]{:S(2)}) collective-permute-start(bf16[2,8,4096]{2,1,0:T(8,128)(2,1)S(1)} %collective-permute-done.4), channel_id=1, source_target_pairs={{0,1},{1,2},{2,3},{3,4},{4,5},{5,6},{6,7},{7,0},{8,9},{9,10},{10,1... | collective-permute-start | bytes 393224 | tf_op jit(solution)/shard_map/ppermute | solution.py:16
  147.2 1.2 copy-start.1
  148.4 167.0 %all-gather.5.cloned.1.call-start = ((), (), s32[]{:S(2)}) async-start(), calls=%async_computation.6 | async-start | bytes 8519680 | tf_op jit(solution)/shard_map/all_gather | solution.py:92
  149.0 318.0 %reduce-scatter.10.cloned.1.call-start = ((), (), s32[]{:S(2)}) async-start(), calls=%async_computation.8 | async-start | bytes 2129920
  229.5 282.2 %reduce-scatter.8.cloned.1.call-start = ((), (), s32[]{:S(2)}) async-start(), calls=%async_computation.7 | async-start | bytes 1179648 | tf_op jit(solution)/shard_map/reduce_scatter | solution.py:97
Sparse Core Ops, SparseCore 0:
  11.3 87.7 all-gather.2
  104.0 41.0 reduce-scatter.5
  148.5 78.0 all-reduce.1
  230.4 84.9 all-gather.4
  319.9 147.0 reduce-scatter.9
  469.6 42.1 reduce-scatter.7
